TPU v7x, 512 devices: a whole 4x4x16 slice. The times are simulated.
512 devices in a mesh: samp: 128 (over z, y, core), cell: 4 (over x).
Axes of the slice: x: 4, y: 4, z: 16, core: 2. Of those that a mesh axis runs over, the one named last changes fastest.
Arguments:
- points: float32 [24, 262144], P(None, 'samp'), may hold values from -1 to 1
- yields: bfloat16 [262144, 1024], P('samp', 'cell'), may hold values from -6 to 6
- term_index: int32 [512, 2], replicated, may hold values from 0 to 95, as said below
- block_group: int32 [8], replicated, may hold values from 0 to 7
Outputs:
- coefficients: float32 [512, 1024], P('cell')
- sobol: float32 [8, 1024], P(None, 'cell')
Inputs may be any that keep to these rules, and one draw needn't show every extreme that they name: `term_index`: row 0 is 0, 0 (the constant term); every other row names one parameter with degree 1 to 3 and column 0, or two different parameters with degrees 1 to 3 each, the lower column first; no two rows are the same.
All inputs are finite; a program needn't handle non-finite values.
Results may differ from a plain program's by a relative error of at most 0.0037.
Values sent between devices are 32-bit elements; how exact they have to be, the bound alone decides.
A program may use at most 64 MiB of HBM per device.

v0:
```python
import jax
import jax.numpy as jnp
from jax import lax
from jax.sharding import PartitionSpec as P

BLOCK = 64
GROUPS = 8


def basis_rows(xs):
    ones = jnp.ones_like(xs)
    first = 1.7320508075688772 * xs
    second = 2.23606797749979 * (1.5 * xs * xs - 0.5)
    third = 2.6457513110645907 * (2.5 * xs * xs * xs - 1.5 * xs)
    stacked = jnp.stack([ones, first, second, third], axis=1)
    return stacked.reshape(4 * xs.shape[0], xs.shape[1])


def design(xs, term_index):
    table = basis_rows(xs)
    left = jnp.take(table, term_index[:, 0], axis=0)
    right = jnp.take(table, term_index[:, 1], axis=0)
    return (left * right).astype(jnp.bfloat16)


def on_device(points, yields, term_index, block_group):
    psi = design(points, term_index)
    cross_local = jnp.dot(psi, yields, preferred_element_type=jnp.float32)
    gram_local = jnp.dot(psi, psi.T, preferred_element_type=jnp.float32)
    gram, cross = lax.psum((gram_local, cross_local), "samp")
    lower = jnp.linalg.cholesky(gram)
    inner = lax.linalg.triangular_solve(lower, cross, left_side=True, lower=True)
    coef = lax.linalg.triangular_solve(lower, inner, left_side=True, lower=True, transpose_a=True)
    total_samples = points.shape[1] * lax.axis_size("samp")
    scaled = coef * jnp.sqrt(jnp.float32(total_samples))
    terms = coef.shape[0]
    keep = (jnp.arange(terms) >= 1).astype(jnp.float32)
    squares = coef * coef * keep[:, None]
    groups = jnp.repeat(block_group, BLOCK)
    member = (groups[None, :] == jnp.arange(GROUPS, dtype=jnp.int32)[:, None]).astype(jnp.float32)
    part = jnp.dot(member, squares, precision=lax.Precision.HIGHEST)
    total = jnp.sum(squares, axis=0)
    sobol = part / total[None, :]
    coefficients = lax.all_to_all(scaled, "cell", split_axis=0, concat_axis=1, tiled=True)
    return (coefficients, sobol)


def solution(mesh):
    placed = (P(None, "samp"), P("samp", "cell"), P(), P())
    return jax.shard_map(
        on_device,
        mesh=mesh,
        in_specs=placed,
        out_specs=(P("cell", None), P(None, "cell")),
        check_vma=False,
    )
```

profile of v0, /device:TPU:8, one launch (start us, length us, event | category | flops | bytes accessed | tf_op | source)
XLA Modules:
  0.0 542.7 jit_solution(15287291031429529462)
XLA Ops:
  7.2 0.8 fusion.59
  8.0 1.0 multiply_bitcast_fusion
  9.1 0.1 pad_maximum_fusion
  9.2 0.5 copy.6
  9.7 0.3 reshape.68
  10.0 3.6 gather_fusion
  13.6 3.6 gather_fusion.1
  17.2 4.0 fusion
  21.2 2.3 fusion.60
  23.6 1.5 fusion.61
  25.1 350.2 %all-reduce.4.cloned.1.call-done = (f32[512,256]{1,0:T(8,128)}, f32[512,512]{0,1:T(8,128)}) async-done(((f32[512,256]{1,0:T(8,128)}, f32[512,512]{0,1:T(8,128)}), (f32[512,256]{1,0:T(8,128)}, f32[512,512]{0,1:T(8,128)})) %all-reduce.4.cloned.1.call-update) | async-done | bytes 1572880 | tf_op jit(solution)/shard_map/psum | solution.py:30
  375.3 1.6 copy.8
  376.8 1.5 fusion.1
  378.3 11.7 %cholesky.104 = f32[128,128]{1,0:T(8,128)S(1)} custom-call(f32[128,128]{1,0:T(8,128)S(1)} %cholesky.266), custom_call_target="Cholesky" | custom-call | tf_op jit(solution)/shard_map/jit(cholesky)/cholesky | solution.py:31
  390.1 0.1 cholesky.224
  390.2 9.8 %custom-call.32 = f32[1,128,128]{1,2,0:T(8,128)S(1)} custom-call(f32[1,128,128]{2,1,0:T(8,128)S(1)} %get-tuple-element.37), custom_call_target="InvertDiagBlocksLowerTriangular" | custom-call | tf_op jit(solution)/shard_map/jit(cholesky)/cholesky | solution.py:31
  400.0 0.3 constant_dynamic-update-slice_fusion.3
  400.3 0.3 convolution_subtract_fusion
  400.7 11.9 %cholesky.217 = f32[128,128]{1,0:T(8,128)S(1)} custom-call(f32[128,128]{1,0:T(8,128)S(1)} %cholesky.270), custom_call_target="Cholesky" | custom-call | tf_op jit(solution)/shard_map/jit(cholesky)/cholesky | solution.py:31
  412.6 0.7 compare_reduce_fusion.2
  413.3 0.6 compare_reduce_fusion.3
  414.0 9.8 %custom-call.33 = f32[1,128,128]{1,2,0:T(8,128)S(1)} custom-call(f32[1,128,128]{2,1,0:T(8,128)S(1)} %get-tuple-element.34), custom_call_target="InvertDiagBlocksLowerTriangular" | custom-call | tf_op jit(solution)/shard_map/jit(cholesky)/cholesky | solution.py:31
  423.8 0.3 convolution_dynamic-update-slice_fusion
  424.1 0.4 convolution_subtract_fusion.5
  424.5 11.7 %cholesky.238 = f32[128,128]{1,0:T(8,128)S(1)} custom-call(f32[128,128]{1,0:T(8,128)S(1)} %cholesky.275), custom_call_target="Cholesky" | custom-call | tf_op jit(solution)/shard_map/jit(cholesky)/cholesky | solution.py:31
  436.2 0.6 compare_reduce_fusion.1
  436.8 9.8 %custom-call.34 = f32[1,128,128]{1,2,0:T(8,128)S(1)} custom-call(f32[1,128,128]{2,1,0:T(8,128)S(1)} %get-tuple-element.31), custom_call_target="InvertDiagBlocksLowerTriangular" | custom-call | tf_op jit(solution)/shard_map/jit(cholesky)/cholesky | solution.py:31
  446.7 0.2 convolution_dynamic-update-slice_fusion.1
  446.9 0.4 convolution_subtract_fusion.8
  447.3 11.9 %cholesky.255 = f32[128,128]{1,0:T(8,128)S(1)} custom-call(f32[128,128]{1,0:T(8,128)S(1)} %convolution_subtract_fusion.8), custom_call_target="Cholesky" | custom-call | tf_op jit(solution)/shard_map/jit(cholesky)/cholesky | solution.py:31
  459.2 0.7 compare_reduce_fusion
  462.4 0.1 select_select_fusion
  462.6 10.9 %while.1 = (s32[]{:T(128)}, f32[512,512]{1,0:T(8,128)S(1)}, s32[4,2]{0,1:T(2,128)S(1)}, f32[4,128,128]{2,1,0:T(8,128)}, s32[]{:T(128)}) while((s32[]{:T(128)}, f32[512,512]{1,0:T(8,128)S(1)}, s32[4,2]{0,1:T(2,128)S(1)}, f32[4,128,128]{2,1,0:T(8,128)}, s32[]{:T(128)}) %tuple.36), condition=%wide.while_cond, body=%wide.while_body.sunk | while | flops 2 | bytes 132705 | solution.py:33
  462.6 0.1 constant_dynamic-slice_fusion.2
  462.7 0.6 fusion.77
  463.3 2.0 bitcast_dynamic-update-slice_fusion.2
  465.3 0.1 constant_dynamic-slice_fusion.2
  465.4 0.6 fusion.77
  466.0 2.0 bitcast_dynamic-update-slice_fusion.2
  468.1 0.6 fusion.77
  468.7 2.0 bitcast_dynamic-update-slice_fusion.2
  470.8 0.6 fusion.77
  471.4 2.1 bitcast_dynamic-update-slice_fusion.2
  473.5 40.1 %custom-call.35 = f32[4,128,128]{1,2,0:T(8,128)S(1)} custom-call(f32[4,128,128]{2,1,0:T(8,128)} %get-tuple-element.10), custom_call_target="InvertDiagBlocksLowerTriangular" | custom-call | tf_op jit(solution)/shard_map/triangular_solve | solution.py:33
  513.6 1.2 fusion.33
  514.8 1.2 convolution_subtract_fusion.7
  516.0 0.3 fusion.46
  516.3 1.2 convolution_subtract_fusion.4
  517.5 0.3 fusion.48
  517.8 1.3 convolution_subtract_fusion.3
  519.1 0.3 fusion.50
  519.4 0.3 fusion.49
  519.7 0.3 convolution_subtract_fusion.6
  520.0 0.3 fusion.47
  520.3 0.4 convolution_subtract_fusion.2
  520.7 0.3 fusion.45
  521.0 0.5 convolution_subtract_fusion.1
  521.5 0.3 fusion.44
  521.8 0.9 fusion.2
  522.6 4.3 all-to-all-start
  526.9 0.1 eq.15
  527.0 1.0 convolution_divide_fusion
  528.0 7.0 %all-to-all-done = f32[4,128,256]{2,1,0:T(8,128)S(1)} async-done(((f32[4,128,256]{2,1,0:T(8,128)}), f32[4,128,256]{2,1,0:T(8,128)S(1)}, u32[]{:S(2)}, u32[]{:S(2)}) %all-to-all-start) | async-done | bytes 524320 | tf_op jit(solution)/shard_map/all_to_all | solution.py:44
  535.0 0.8 copy.11
  (26 shorter events, 0.5 us)
Async XLA Ops:
  7.2 16.4 %copy-start = (bf16[2048,256]{1,0:T(8,128)(2,1)S(1)}, bf16[2048,256]{1,0:T(8,128)(2,1)}, u32[]{:S(2)}) copy-start(bf16[2048,256]{1,0:T(8,128)(2,1)} %param.7) | copy-start | bytes 3145732
  7.2 368.1 %all-reduce.4.cloned.1.call-start = ((), (), s32[]{:S(2)}) async-start(), calls=%async_computation.1 | async-start | bytes 3145728 | tf_op jit(solution)/shard_map/psum | solution.py:30
  514.8 12.1 %copy-start.1 = (s32[8]{0:T(128)S(1)}, s32[8]{0:T(128)}, u32[]{:S(2)}) copy-start(s32[8]{0:T(128)} %param.9) | copy-start | bytes 100
  522.6 12.3 %all-to-all-start = ((f32[4,128,256]{2,1,0:T(8,128)}), f32[4,128,256]{2,1,0:T(8,128)S(1)}, u32[]{:S(2)}, u32[]{:S(2)}) async-start(f32[4,128,256]{2,1,0:T(8,128)} %bitcast.16), calls=%async_computation | async-start | bytes 1048576 | tf_op jit(solution)/shard_map/all_to_all | solution.py:44
Sparse Core Ops, SparseCore 0:
  25.2 350.0 all-reduce.3
where the time goes:
time: 543 us
  waiting for transfers between devices  357 us (66%)
  other arithmetic  127 us (23%)
  local copies, waits for them, and re-layouts  22.3 us (4%)
  between operations  16.9 us (3%)
  matrix products  14.7 us (3%)
    psum x1, waiting for transfers between devices, on_device(): gram, cross = lax.psum((gram_local, cross_local), 'samp')  350 us
    another operation x15, other arithmetic, on_device(): lower = jnp.linalg.cholesky(gram)  79.5 us
    another operation x3, other arithmetic, on_device(): lax.linalg.triangular_solve(lower, inner, left_side=True, lower=True, tra...  40.3 us
    another operation x12, local copies, waits for them, and re-layouts  10.9 us
  transfers between devices with their start and end apart: 2, of which 2 were waited for; matrix products, arithmetic and copies ran while one was open for 0% of the time, Pallas kernels for 0%

commit v1 on v0

--- a/solution.py
+++ b/solution.py
@@ -41,7 +41,16 @@
     part = jnp.dot(member, squares, precision=lax.Precision.HIGHEST)
     total = jnp.sum(squares, axis=0)
     sobol = part / total[None, :]
-    coefficients = lax.all_to_all(scaled, "cell", split_axis=0, concat_axis=1, tiled=True)
+    make_the_area = lambda view: jnp.concatenate(
+        lax.all_to_all(
+            jnp.stack(jnp.split(view, lax.axis_size("cell"), axis=0), axis=0),
+            axis_name="cell",
+            split_axis=0,
+            concat_axis=0,
+        ),
+        axis=1,
+    )
+    coefficients = make_the_area(scaled)
     return (coefficients, sobol)
 
 

time: 543 us -> 547 us (level)
  no operation moved by 1% of the time
where the time goes in v1:
time: 547 us; the launch traced here: 543 us
  waiting for transfers between devices  357 us (65%)
  other arithmetic  128 us (23%)
  local copies, waits for them, and re-layouts  22.9 us (4%)
  between operations  17.1 us (3%)
  matrix products  14.7 us (3%)
    psum x1, waiting for transfers between devices, on_device(): gram, cross = lax.psum((gram_local, cross_local), 'samp')  350 us
    another operation x15, other arithmetic, on_device(): lower = jnp.linalg.cholesky(gram)  79.7 us
    another operation x3, other arithmetic, on_device(): lax.linalg.triangular_solve(lower, inner, left_side=True, lower=True, tra...  40.3 us
  transfers between devices with their start and end apart: 2, of which 2 were waited for; matrix products, arithmetic and copies ran while one was open for 0% of the time, Pallas kernels for 0%

profile of v1, /device:TPU:8, one launch (start us, length us, event | category | flops | bytes accessed | tf_op | source)
XLA Modules:
  0.0 543.3 jit_solution(17221552858641622813)
XLA Ops:
  7.2 0.8 fusion.59
  8.0 1.0 multiply_bitcast_fusion
  9.1 0.1 pad_maximum_fusion
  9.2 0.5 copy.9
  9.7 0.3 reshape.68
  10.0 3.6 gather_fusion
  13.6 3.8 gather_fusion.1
  17.4 4.0 fusion
  21.5 2.3 fusion.60
  23.8 1.5 fusion.61
  25.4 349.6 %all-reduce.4.cloned.1.call-done = (f32[512,256]{1,0:T(8,128)}, f32[512,512]{0,1:T(8,128)}) async-done(((f32[512,256]{1,0:T(8,128)}, f32[512,512]{0,1:T(8,128)}), (f32[512,256]{1,0:T(8,128)}, f32[512,512]{0,1:T(8,128)})) %all-reduce.4.cloned.1.call-update) | async-done | bytes 1572880 | tf_op jit(solution)/shard_map/psum | solution.py:30
  375.0 1.6 copy.11
  376.6 1.5 fusion.1
  378.1 11.7 %cholesky.104 = f32[128,128]{1,0:T(8,128)S(1)} custom-call(f32[128,128]{1,0:T(8,128)S(1)} %cholesky.266), custom_call_target="Cholesky" | custom-call | tf_op jit(solution)/shard_map/jit(cholesky)/cholesky | solution.py:31
  389.8 0.1 cholesky.224
  389.9 9.8 %custom-call.32 = f32[1,128,128]{1,2,0:T(8,128)S(1)} custom-call(f32[1,128,128]{2,1,0:T(8,128)S(1)} %get-tuple-element.43), custom_call_target="InvertDiagBlocksLowerTriangular" | custom-call | tf_op jit(solution)/shard_map/jit(cholesky)/cholesky | solution.py:31
  399.8 0.3 constant_dynamic-update-slice_fusion.3
  400.1 0.3 convolution_subtract_fusion
  400.4 12.2 %cholesky.217 = f32[128,128]{1,0:T(8,128)S(1)} custom-call(f32[128,128]{1,0:T(8,128)S(1)} %cholesky.270), custom_call_target="Cholesky" | custom-call | tf_op jit(solution)/shard_map/jit(cholesky)/cholesky | solution.py:31
  412.6 0.7 compare_reduce_fusion.2
  413.3 0.6 compare_reduce_fusion.3
  414.0 9.8 %custom-call.33 = f32[1,128,128]{1,2,0:T(8,128)S(1)} custom-call(f32[1,128,128]{2,1,0:T(8,128)S(1)} %get-tuple-element.40), custom_call_target="InvertDiagBlocksLowerTriangular" | custom-call | tf_op jit(solution)/shard_map/jit(cholesky)/cholesky | solution.py:31
  423.8 0.3 convolution_dynamic-update-slice_fusion
  424.0 0.4 convolution_subtract_fusion.5
  424.5 11.7 %cholesky.238 = f32[128,128]{1,0:T(8,128)S(1)} custom-call(f32[128,128]{1,0:T(8,128)S(1)} %cholesky.275), custom_call_target="Cholesky" | custom-call | tf_op jit(solution)/shard_map/jit(cholesky)/cholesky | solution.py:31
  436.2 0.6 compare_reduce_fusion.1
  436.8 9.8 %custom-call.34 = f32[1,128,128]{1,2,0:T(8,128)S(1)} custom-call(f32[1,128,128]{2,1,0:T(8,128)S(1)} %get-tuple-element.37), custom_call_target="InvertDiagBlocksLowerTriangular" | custom-call | tf_op jit(solution)/shard_map/jit(cholesky)/cholesky | solution.py:31
  446.6 0.2 convolution_dynamic-update-slice_fusion.1
  446.9 0.4 convolution_subtract_fusion.8
  447.2 11.9 %cholesky.255 = f32[128,128]{1,0:T(8,128)S(1)} custom-call(f32[128,128]{1,0:T(8,128)S(1)} %convolution_subtract_fusion.8), custom_call_target="Cholesky" | custom-call | tf_op jit(solution)/shard_map/jit(cholesky)/cholesky | solution.py:31
  459.2 0.7 compare_reduce_fusion
  462.4 0.1 select_select_fusion
  462.5 10.9 %while.1 = (s32[]{:T(128)}, f32[512,512]{1,0:T(8,128)S(1)}, s32[4,2]{0,1:T(2,128)S(1)}, f32[4,128,128]{2,1,0:T(8,128)}, s32[]{:T(128)}) while((s32[]{:T(128)}, f32[512,512]{1,0:T(8,128)S(1)}, s32[4,2]{0,1:T(2,128)S(1)}, f32[4,128,128]{2,1,0:T(8,128)}, s32[]{:T(128)}) %tuple.40), condition=%wide.while_cond, body=%wide.while_body.sunk | while | flops 2 | bytes 132705 | solution.py:33
  462.6 0.6 fusion.77
  463.2 2.0 bitcast_dynamic-update-slice_fusion.2
  465.3 0.6 fusion.77
  465.9 2.0 bitcast_dynamic-update-slice_fusion.2
  468.0 0.6 fusion.77
  468.6 2.0 bitcast_dynamic-update-slice_fusion.2
  470.7 0.6 fusion.77
  471.3 2.1 bitcast_dynamic-update-slice_fusion.2
  473.4 40.1 %custom-call.35 = f32[4,128,128]{1,2,0:T(8,128)S(1)} custom-call(f32[4,128,128]{2,1,0:T(8,128)} %get-tuple-element.10), custom_call_target="InvertDiagBlocksLowerTriangular" | custom-call | tf_op jit(solution)/shard_map/triangular_solve | solution.py:33
  513.5 1.2 fusion.33
  514.7 1.2 convolution_subtract_fusion.7
  515.9 0.3 fusion.46
  516.2 1.2 convolution_subtract_fusion.4
  517.4 0.3 fusion.48
  517.8 1.3 convolution_subtract_fusion.3
  519.1 0.3 fusion.50
  519.4 0.3 fusion.49
  519.6 0.3 convolution_subtract_fusion.6
  520.0 0.3 fusion.47
  520.2 0.4 convolution_subtract_fusion.2
  520.6 0.3 fusion.45
  520.9 0.5 convolution_subtract_fusion.1
  521.4 0.3 fusion.44
  521.7 0.1 fusion.2
  521.9 0.8 pad_maximum_fusion.2
  522.7 4.2 all-to-all-start
  527.0 0.1 eq.15
  527.1 1.0 convolution_divide_fusion
  528.1 7.0 %all-to-all-done = f32[4,128,256]{2,1,0:T(8,128)S(1)} async-done(((f32[4,128,256]{2,1,0:T(8,128)}), f32[4,128,256]{2,1,0:T(8,128)S(1)}, u32[]{:S(2)}, u32[]{:S(2)}) %all-to-all-start) | async-done | bytes 524320 | tf_op jit(solution)/shard_map/all_to_all | solution.py:45
  535.0 0.2 copy.12
  535.2 1.0 copy.13
  (29 shorter events, 0.7 us)
Async XLA Ops:
  7.2 16.6 %copy-start = (bf16[2048,256]{1,0:T(8,128)(2,1)S(1)}, bf16[2048,256]{1,0:T(8,128)(2,1)}, u32[]{:S(2)}) copy-start(bf16[2048,256]{1,0:T(8,128)(2,1)} %param.7) | copy-start | bytes 3145732
  7.2 367.8 %all-reduce.4.cloned.1.call-start = ((), (), s32[]{:S(2)}) async-start(), calls=%async_computation.1 | async-start | bytes 3145728 | tf_op jit(solution)/shard_map/psum | solution.py:30
  517.7 9.2 %copy-start.1 = (s32[8]{0:T(128)S(1)}, s32[8]{0:T(128)}, u32[]{:S(2)}) copy-start(s32[8]{0:T(128)} %param.9) | copy-start | bytes 100
  522.7 12.3 %all-to-all-start = ((f32[4,128,256]{2,1,0:T(8,128)}), f32[4,128,256]{2,1,0:T(8,128)S(1)}, u32[]{:S(2)}, u32[]{:S(2)}) async-start(f32[4,128,256]{2,1,0:T(8,128)} %pad_maximum_fusion.2), calls=%async_computation | async-start | bytes 1048576 | tf_op jit(solution)/shard_map/all_to_all | solution.py:45
Sparse Core Ops, SparseCore 0:
  25.5 349.4 all-reduce.3
